TPU v7x, 256 devices: a whole 4x4x8 slice. The times are simulated.
256 devices in a mesh: node: 16 (over z_lo, y), rep: 16 (over x, z_hi, core).
Axes of the slice: x: 4, y: 4, z: 8 (z_hi: 2, z_lo: 4; z = z_hi * 4 + z_lo), core: 2. Of those that a mesh axis runs over, the one named last changes fastest.
Arguments:
- tokens: bfloat16 [32768, 8192], P(('node', 'rep')), may hold values from -24 to 24
- norm_gain: float32 [8192], replicated, may hold values from 0.5 to 1.5
- key_cotangent: bfloat16 [32768, 512], P(('node', 'rep')), may hold values from -6 to 6
- secondary: bfloat16 [8192, 512], P('node'), may hold values from -0.0625 to 0.0625
- master: float32 [8192, 512], P(('node', 'rep')), may hold values from -0.0625 to 0.0625
- moment_first: float32 [4096, 1024], P(('node', 'rep')), may hold values from -0.03314563 to 0.03314563
- moment_second: float32 [4096, 1024], P(('node', 'rep')), may hold values from 7.6293945e-06 to 0.00012207031
- signs: int32 [1024], replicated, may hold values from 0 to 1
Outputs:
- keys: bfloat16 [32768, 512], P(('node', 'rep'))
- token_grad: bfloat16 [32768, 8192], P(('node', 'rep'))
- new_master: float32 [8192, 512], P(('node', 'rep'))
- new_first: float32 [4096, 1024], P(('node', 'rep'))
- new_second: float32 [4096, 1024], P(('node', 'rep'))
- new_secondary: bfloat16 [8192, 512], P('node')
All inputs are finite; a program needn't handle non-finite values.
Results may differ from a plain program's by a relative error of at most 0.0049.
Values may be sent and summed in bfloat16 or wider, within the bound.
No kernel may reach another device: no remote copies, remote signals or barrier semaphores. Data moves between devices by JAX's collectives and lax.ppermute only.
A program may use at most 128 MiB of HBM per device.

v0:
```python
import math
import jax
import jax.numpy as jnp
from jax import lax
from jax.sharding import PartitionSpec as P

PAIR_GAP = 16
norm_eps = 1e-05
adam_eps = 1e-08
beta_first = 0.9
beta_second = 0.95
adam_steps = 10
learn_rate = 0.002
weight_decay = 0.1


def split_up(value, dim, peers):
    dims = value.shape
    blocks = value.reshape(*dims[:dim], peers, dims[dim] // peers, *dims[dim + 1 :])
    return jnp.moveaxis(blocks, dim, 0)


def sent_and_summed(value, axis, dim):
    peers = lax.axis_size(axis)
    blocks = lax.all_to_all(split_up(value, dim, peers), axis, 0, 0, tiled=True)
    return jnp.sum(blocks.astype(jnp.float32), axis=0)


def sent_to_all(value, axis):
    copies = jnp.broadcast_to(value, (lax.axis_size(axis), *value.shape))
    return lax.all_to_all(copies, axis, split_axis=0, concat_axis=0, tiled=True)


def laid_out(blocks, dim):
    blocks = jnp.moveaxis(blocks, 0, dim)
    dims = blocks.shape
    return blocks.reshape(*dims[:dim], dims[dim] * dims[dim + 1], *dims[dim + 2 :])


def gathered_copies(value, axis, dim):
    blocks = sent_to_all(value, axis)
    return laid_out(blocks, dim)


def sylvester(extent):
    position = jnp.arange(extent, dtype=jnp.int32)
    parity = jnp.zeros((extent, extent), jnp.int32)
    for bit_place in range(extent.bit_length() - 1):
        parity = parity + (position[:, None] >> bit_place & 1) * (
            position[None, :] >> bit_place & 1
        )
    return (1 - 2 * (parity % 2)).astype(jnp.float32)


def shards(tokens, norm_gain, key_cotangent, secondary, master, moment_first, moment_second, signs):
    tok_rows, model_width = tokens.shape
    key_width = key_cotangent.shape[1]
    node_count = lax.axis_size("node")
    rep_count = lax.axis_size("rep")
    all_tokens = tok_rows * node_count * rep_count
    had_table = sylvester(key_width)
    sign_rows = (1 - 2 * signs).astype(jnp.float32).reshape(2, key_width)
    floats = tokens.astype(jnp.float32)
    inverse = lax.rsqrt(jnp.mean(floats * floats, axis=-1, keepdims=True) + norm_eps)
    normed = floats * inverse
    hidden = (normed * norm_gain).astype(jnp.bfloat16)
    gathered = lax.all_gather(secondary, "node", axis=0, tiled=True)
    keys = jnp.dot(hidden, gathered, preferred_element_type=jnp.float32).astype(jnp.bfloat16)
    hidden_grad = lax.dot_general(
        key_cotangent, gathered, (((1,), (1,)), ((), ())), preferred_element_type=jnp.float32
    )
    scaled = hidden_grad * norm_gain
    token_grad = (
        inverse * (scaled - normed * jnp.mean(scaled * normed, axis=-1, keepdims=True))
    ).astype(jnp.bfloat16)
    rot_scale = 1.0 / (math.sqrt(2 * key_width) * all_tokens)
    flipped = (key_cotangent[:, None, :] * sign_rows.astype(jnp.bfloat16)).reshape(
        2 * tok_rows, key_width
    )
    rotated = (
        jnp.dot(flipped, had_table.astype(jnp.bfloat16), preferred_element_type=jnp.float32)
        * rot_scale
    )
    rotated = rotated.astype(jnp.bfloat16).reshape(tok_rows, 2, key_width)
    amount = lax.axis_size("node") * (model_width // 2 // node_count)
    grouped = hidden.reshape(tok_rows, amount // PAIR_GAP, 2, PAIR_GAP)
    halves = jnp.einsum("tgaj,tak->agjk", grouped, rotated, preferred_element_type=jnp.float32)
    joined = jnp.concatenate([halves[0] + halves[1], halves[0] - halves[1]], axis=-1)
    partial_sum = lax.psum_scatter(
        joined.reshape(amount, 2 * key_width).astype(jnp.bfloat16),
        "node",
        scatter_dimension=0,
        tiled=True,
    )
    coded = sent_and_summed(partial_sum, "rep", 0)
    new_first = beta_first * moment_first + (1.0 - beta_first) * coded
    new_second = beta_second * moment_second + (1.0 - beta_second) * coded * coded
    first_hat = new_first / (1.0 - beta_first**adam_steps)
    second_hat = new_second / (1.0 - beta_second**adam_steps)
    ratio = first_hat / (jnp.sqrt(second_hat) + adam_eps)
    lower = ratio[:, :key_width]
    upper = ratio[:, key_width:]
    norm_root = math.sqrt(2 * key_width)
    row_even = jnp.dot(lower + upper, had_table) / norm_root * sign_rows[0]
    row_odd = jnp.dot(lower - upper, had_table) / norm_root * sign_rows[1]
    stacked = jnp.stack([row_even, row_odd], axis=1)
    master_rows = master.shape[0]
    update = (
        stacked.reshape(master_rows // (2 * PAIR_GAP), PAIR_GAP, 2, key_width)
        .transpose(0, 2, 1, 3)
        .reshape(master_rows, key_width)
    )
    new_master = master - learn_rate * (update + weight_decay * master)
    new_secondary = gathered_copies(new_master.astype(jnp.bfloat16), "rep", 0)
    return (keys, token_grad, new_master, new_first, new_second, new_secondary)


def solution(mesh):
    return jax.shard_map(
        shards,
        mesh=mesh,
        in_specs=(
            P(("node", "rep"), None),
            P(),
            P(("node", "rep"), None),
            P("node", None),
            P(("node", "rep"), None),
            P(("node", "rep"), None),
            P(("node", "rep"), None),
            P(),
        ),
        out_specs=(
            P(("node", "rep"), None),
            P(("node", "rep"), None),
            P(("node", "rep"), None),
            P(("node", "rep"), None),
            P(("node", "rep"), None),
            P("node", None),
        ),
        check_vma=False,
    )
```

profile of v0, /device:TPU:1, one launch (start us, length us, event | category | flops | bytes accessed | tf_op | source)
XLA Modules:
  0.0 313.9 jit_solution(15563459181511982867)
XLA Ops:
  7.2 0.0 all-gather.2.cloned.1.call-start
  7.2 0.7 all-gather.2.cloned.1.call-update
  7.9 0.0 reduce-scatter.2.cloned.1.call-start
  7.9 0.7 subtract_convert_fusion.1
  8.7 1.2 broadcast_multiply_fusion
  9.8 0.1 mul.382
  10.0 0.0 copy-start
  10.0 0.0 copy-start.2
  10.0 0.0 copy-start.3
  10.0 1.4 fusion.11
  11.5 0.1 reshape.197
  11.6 0.0 copy-done
  11.6 0.5 fusion.8
  12.1 104.0 %all-gather.2.cloned.1.call-done = bf16[8192,512]{1,0:T(8,128)(2,1)} async-done(((bf16[512,512]{1,0:T(8,128)(2,1)}), bf16[8192,512]{1,0:T(8,128)(2,1)}) %all-gather.2.cloned.1.call-update) | async-done | bytes 8388624 | tf_op jit(solution)/shard_map/all_gather | solution.py:67
  116.1 0.0 copy-done.2
  116.1 0.0 copy-done.3
  116.1 0.0 copy-start.1
  116.1 6.4 %fusion.4 = (f32[128]{0:T(128)S(1)}, f32[128,8192]{1,0:T(8,128)S(1)}) fusion(bf16[128,8192]{1,0:T(8,128)(2,1)S(1)} %copy-done, f32[128]{0:T(128)S(1)} %add_rsqrt_fusion, f32[8192]{0:T(1024)S(1)} %copy-done.3, bf16[128,512]{1,0:T(8,128)(2,1)S(1)} %copy-done.2, bf16[8192,512]{1,0:T(8,128)(2,1)} %all-gather.2.cloned.1.call-done), kind=kOutput, calls=%fused_computation.10 | convolution fusion | flops 1078984576 | bytes 14844928 | tf_op jit(solution)/shard_map/dot_general | solution.py:69
  122.6 0.0 copy-done.1
  122.6 2.5 fusion.7
  125.1 2.5 copy.16
  127.6 3.9 %fusion.9 = f32[2,256,16,512]{3,1,2,0:T(8,128)S(1)} fusion(bf16[128,256,2,16]{0,3,2,1:T(8,128)(2,1)} %bitcast.28, bf16[128,2,512,1]{2,1,0,3:T(2,128)(2,1)S(1)} %bitcast.30), kind=kOutput, calls=%fused_computation.15 | convolution fusion | flops 1073741824 | bytes 19136512 | tf_op jit(solution)/shard_map/tgaj,tak->agjk/dot_general | solution.py:87
  131.6 4.1 %add_convert_fusion = (bf16[1,256,16,512]{3,1,2,0:T(8,128)(2,1)}, bf16[1,256,16,512]{3,1,2,0:T(8,128)(2,1)S(1)}) fusion(f32[2,256,16,512]{3,1,2,0:T(8,128)S(1)} %fusion.9), kind=kLoop, calls=%fused_computation.3 | loop fusion | flops 8388608 | bytes 25165824 | tf_op jit(solution)/shard_map/convert.3
  135.7 6.5 %copy.19 = bf16[1,256,16,512]{3,2,1,0:T(8,128)(2,1)} copy(bf16[1,256,16,512]{3,1,2,0:T(8,128)(2,1)} %get-tuple-element.11) | data formatting | bytes 8388608 | tf_op jit(solution)/shard_map/convert.3
  142.2 4.3 %copy.20 = bf16[1,256,16,512]{3,2,1,0:T(8,128)(2,1)} copy(bf16[1,256,16,512]{3,1,2,0:T(8,128)(2,1)S(1)} %get-tuple-element.12) | data formatting | bytes 8388608 | tf_op jit(solution)/shard_map/convert.2
  146.5 7.9 %pad_maximum_fusion = bf16[4096,1024]{1,0:T(8,128)(2,1)} fusion(bf16[4096,512]{1,0:T(8,128)(2,1)} %bitcast.27, bf16[4096,512]{1,0:T(8,128)(2,1)} %bitcast.26), kind=kLoop, calls=%fused_computation.1 | loop fusion | flops 16777216 | bytes 16777216 | tf_op jit(solution)/shard_map/concatenate | solution.py:88
  154.4 0.0 copy-start.5
  154.4 0.0 copy-start.6
  154.4 0.0 reduce-scatter.2.cloned.1.call-update
  154.4 96.1 %reduce-scatter.2.cloned.1.call-done = bf16[256,1024]{1,0:T(8,128)(2,1)} async-done(((bf16[4096,1024]{1,0:T(8,128)(2,1)}), bf16[256,1024]{1,0:T(8,128)(2,1)}) %reduce-scatter.2.cloned.1.call-update) | async-done | bytes 524304 | tf_op jit(solution)/shard_map/reduce_scatter | solution.py:89
  250.5 15.8 %all-to-all-start = ((bf16[16,16,1024]{2,1,0:T(8,128)(2,1)}), bf16[16,16,1024]{2,1,0:T(8,128)(2,1)S(1)}, u32[]{:S(2)}, u32[]{:S(2)}) async-start(bf16[16,16,1024]{2,1,0:T(8,128)(2,1)} %bitcast.31), calls=%async_computation.1 | async-start | bytes 1048576 | tf_op jit(solution)/shard_map/all_to_all | solution.py:25
  266.3 13.7 %all-to-all-done = bf16[16,16,1024]{2,1,0:T(8,128)(2,1)S(1)} async-done(((bf16[16,16,1024]{2,1,0:T(8,128)(2,1)}), bf16[16,16,1024]{2,1,0:T(8,128)(2,1)S(1)}, u32[]{:S(2)}, u32[]{:S(2)}) %all-to-all-start) | async-done | bytes 524320 | tf_op jit(solution)/shard_map/all_to_all | solution.py:25
  280.0 0.1 convert_reduce_fusion
  280.1 0.0 copy-done.5
  280.1 0.0 copy-done.6
  280.1 0.7 add_divide_fusion
  280.8 1.3 fusion.13
  282.1 0.0 copy-start.4
  282.1 1.3 fusion.12
  283.4 0.0 copy-done.4
  283.4 0.6 fusion.42
  284.1 0.8 broadcast_in_dim.2
  284.9 7.7 %all-to-all-start.1 = ((bf16[16,32,512]{2,1,0:T(8,128)(2,1)}), bf16[16,32,512]{2,1,0:T(8,128)(2,1)S(1)}, u32[]{:S(2)}, u32[]{:S(2)}) async-start(bf16[16,32,512]{2,1,0:T(8,128)(2,1)} %broadcast_in_dim.2), calls=%async_computation.2 | async-start | bytes 1048576 | tf_op jit(solution)/shard_map/all_to_all | solution.py:31
  292.6 5.3 %convolution_convert_fusion = bf16[128,512]{1,0:T(8,128)(2,1)} fusion(bf16[128,8192]{1,0:T(8,128)(2,1)S(1)} %get-tuple-element.14, bf16[8192,512]{1,0:T(8,128)(2,1)} %all-gather.2.cloned.1.call-done), kind=kOutput, calls=%fused_computation.22 | convolution fusion | flops 1073807360 | bytes 10616832 | tf_op jit(solution)/shard_map/dot_general | solution.py:68
  297.9 8.4 %all-to-all-done.1 = bf16[16,32,512]{2,1,0:T(8,128)(2,1)S(1)} async-done(((bf16[16,32,512]{2,1,0:T(8,128)(2,1)}), bf16[16,32,512]{2,1,0:T(8,128)(2,1)S(1)}, u32[]{:S(2)}, u32[]{:S(2)}) %all-to-all-start.1) | async-done | bytes 524320 | tf_op jit(solution)/shard_map/all_to_all | solution.py:31
  306.3 0.8 copy.29
  (10 shorter events, 0.1 us)
Async XLA Ops:
  7.2 108.9 %all-gather.2.cloned.1.call-start = ((), (), s32[]{:S(2)}) async-start(), calls=%async_computation.3 | async-start | bytes 8912896 | tf_op jit(solution)/shard_map/all_gather | solution.py:67
  7.9 242.6 %reduce-scatter.2.cloned.1.call-start = ((), (), s32[]{:S(2)}) async-start(), calls=%async_computation.4 | async-start | bytes 8912896 | tf_op jit(solution)/shard_map/reduce_scatter | solution.py:89
  10.0 1.6 copy-start
  10.0 106.1 %copy-start.2 = (bf16[128,512]{1,0:T(8,128)(2,1)S(1)}, bf16[128,512]{1,0:T(8,128)(2,1)}, u32[]{:S(2)}) copy-start(bf16[128,512]{1,0:T(8,128)(2,1)} %param.10) | copy-start | bytes 393220
  10.0 106.1 %copy-start.3 = (f32[8192]{0:T(1024)S(1)}, f32[8192]{0:T(1024)}, u32[]{:S(2)}) copy-start(f32[8192]{0:T(1024)} %param.9) | copy-start | bytes 98308
  116.1 6.5 %copy-start.1 = (bf16[128,8192]{1,0:T(8,128)(2,1)S(1)}, bf16[128,8192]{1,0:T(8,128)(2,1)}, u32[]{:S(2)}) copy-start(bf16[128,8192]{1,0:T(8,128)(2,1)} %param.8) | copy-start | bytes 6291460
  154.4 125.7 %copy-start.5 = (f32[16,1024]{1,0:T(8,128)S(1)}, f32[16,1024]{1,0:T(8,128)}, u32[]{:S(2)}) copy-start(f32[16,1024]{1,0:T(8,128)} %param.13) | copy-start | bytes 196612
  154.4 125.7 %copy-start.6 = (f32[16,1024]{1,0:T(8,128)S(1)}, f32[16,1024]{1,0:T(8,128)}, u32[]{:S(2)}) copy-start(f32[16,1024]{1,0:T(8,128)} %param.14) | copy-start | bytes 196612
  250.5 29.5 %all-to-all-start = ((bf16[16,16,1024]{2,1,0:T(8,128)(2,1)}), bf16[16,16,1024]{2,1,0:T(8,128)(2,1)S(1)}, u32[]{:S(2)}, u32[]{:S(2)}) async-start(bf16[16,16,1024]{2,1,0:T(8,128)(2,1)} %bitcast.31), calls=%async_computation.1 | async-start | bytes 1048576 | tf_op jit(solution)/shard_map/all_to_all | solution.py:25
  282.1 1.3 copy-start.4
  284.9 21.4 %all-to-all-start.1 = ((bf16[16,32,512]{2,1,0:T(8,128)(2,1)}), bf16[16,32,512]{2,1,0:T(8,128)(2,1)S(1)}, u32[]{:S(2)}, u32[]{:S(2)}) async-start(bf16[16,32,512]{2,1,0:T(8,128)(2,1)} %broadcast_in_dim.2), calls=%async_computation.2 | async-start | bytes 1048576 | tf_op jit(solution)/shard_map/all_to_all | solution.py:31
Sparse Core Ops, SparseCore 0:
  9.8 106.2 all-gather.1
  154.5 95.9 reduce-scatter.1
where the time goes:
time: 314 us
  waiting for transfers between devices  223 us (71%)
  starting transfers between devices  23.6 us (8%)
  matrix products  19.7 us (6%)
  other arithmetic  18.3 us (6%)
  local copies, waits for them, and re-layouts  15.2 us (5%)
  between operations  14.2 us (5%)
    all_gather x1, waiting for transfers between devices, shards(): gathered = lax.all_gather(secondary, 'node', axis=0, tiled=True)  104 us
    reduce_scatter x1, waiting for transfers between devices, shards(): lax.psum_scatter(joined.reshape(amount, 2 * key_width).astype(jnp.bfloat1...  96.1 us
    all_to_all x1, starting transfers between devices, sent_and_summed(): blocks = lax.all_to_all(split_up(value, dim, peers), axis, 0, 0, tiled=True)  15.8 us
    all_to_all x1, waiting for transfers between devices, sent_and_summed(): blocks = lax.all_to_all(split_up(value, dim, peers), axis, 0, 0, tiled=True)  13.7 us
    another operation x2, local copies, waits for them, and re-layouts  10.8 us
    all_to_all x1, waiting for transfers between devices, sent_to_all(): return lax.all_to_all(copies, axis, split_axis=0, concat_axis=0, tiled=True)  8.4 us
    concatenate x1, other arithmetic, shards(): jnp.concatenate([halves[0] + halves[1], halves[0] - halves[1]], axis=-1)  7.88 us
    all_to_all x1, starting transfers between devices, sent_to_all(): return lax.all_to_all(copies, axis, split_axis=0, concat_axis=0, tiled=True)  7.7 us
  transfers between devices with their start and end apart: 4, of which 4 were waited for; matrix products, arithmetic and copies ran while one was open for 3% of the time, Pallas kernels for 0%

commit v1 on v0

--- a/solution.py
+++ b/solution.py
@@ -64,7 +64,10 @@
     inverse = lax.rsqrt(jnp.mean(floats * floats, axis=-1, keepdims=True) + norm_eps)
     normed = floats * inverse
     hidden = (normed * norm_gain).astype(jnp.bfloat16)
-    gathered = lax.all_gather(secondary, "node", axis=0, tiled=True)
+    count = lax.axis_size("node")
+    pieces = jnp.stack([secondary for _ in range(count)])
+    pieces = lax.all_to_all(pieces, "node", split_axis=0, concat_axis=0)
+    gathered = jnp.concatenate(pieces, axis=0)
     keys = jnp.dot(hidden, gathered, preferred_element_type=jnp.float32).astype(jnp.bfloat16)
     hidden_grad = lax.dot_general(
         key_cotangent, gathered, (((1,), (1,)), ((), ())), preferred_element_type=jnp.float32

time: 314 us -> 407 us (1.30)
  waiting for transfers between devices: 223 us -> 303 us
  starting transfers between devices: 23.6 us -> 32.6 us
  local copies, waits for them, and re-layouts: 15.2 us -> 20.3 us
    all_to_all x0 -> x1, waiting for transfers between devices: none -> 149 us  [shards(): pieces = lax.all_to_all(pieces, 'node', split_axis=0, concat_axis=0)]
    all_gather x1 -> x0, waiting for transfers between devices: 104 us -> none  [shards(): gathered = lax.all_gather(secondary, 'node', axis=0, tiled=True)]
    reduce_scatter x1, waiting for transfers between devices: 96.1 us -> 132 us  [shards(): lax.psum_scatter(joined.reshape(amount, 2 * key_width).astype(jnp.bfloat1...]
    all_to_all x0 -> x1, starting transfers between devices: none -> 9.37 us  [shards(): pieces = lax.all_to_all(pieces, 'node', split_axis=0, concat_axis=0)]
    another operation x2 -> x3, local copies, waits for them, and re-layouts: 10.8 us -> 15.9 us
  transfers between devices with their start and end apart: 4 -> 4, of which waited for: 4 -> 4; matrix products, arithmetic and copies ran while one was open for 3% -> 2% of each run, Pallas kernels for 0% -> 0%
where the time goes in v1:
time: 407 us; the launch traced here: 406 us
  waiting for transfers between devices  303 us (74%)
  starting transfers between devices  32.6 us (8%)
  local copies, waits for them, and re-layouts  20.3 us (5%)
  matrix products  19.7 us (5%)
  other arithmetic  16.7 us (4%)
  between operations  14.2 us (3%)
    all_to_all x1, waiting for transfers between devices, shards(): pieces = lax.all_to_all(pieces, 'node', split_axis=0, concat_axis=0)  149 us
    reduce_scatter x1, waiting for transfers between devices, shards(): lax.psum_scatter(joined.reshape(amount, 2 * key_width).astype(jnp.bfloat1...  132 us
    all_to_all x1, starting transfers between devices, sent_and_summed(): blocks = lax.all_to_all(split_up(value, dim, peers), axis, 0, 0, tiled=True)  15.2 us
    all_to_all x1, waiting for transfers between devices, sent_and_summed(): blocks = lax.all_to_all(split_up(value, dim, peers), axis, 0, 0, tiled=True)  13.7 us
    another operation x2, local copies, waits for them, and re-layouts  10.8 us
    all_to_all x1, starting transfers between devices, shards(): pieces = lax.all_to_all(pieces, 'node', split_axis=0, concat_axis=0)  9.37 us
    all_to_all x1, waiting for transfers between devices, sent_to_all(): return lax.all_to_all(copies, axis, split_axis=0, concat_axis=0, tiled=True)  8.4 us
  transfers between devices with their start and end apart: 4, of which 4 were waited for; matrix products, arithmetic and copies ran while one was open for 2% of the time, Pallas kernels for 0%

profile of v1, /device:TPU:1, one launch (start us, length us, event | category | flops | bytes accessed | tf_op | source)
XLA Modules:
  0.0 406.1 jit_solution(3157900160021128071)
XLA Ops:
  7.2 5.1 %stack.8 = bf16[16,512,512]{2,1,0:T(8,128)(2,1)} broadcast(bf16[512,512]{1,0:T(8,128)(2,1)} %param.11), dimensions={1,2} | broadcast | bytes 8912896 | tf_op jit(solution)/shard_map/stack | solution.py:68
  12.3 0.0 copy-start.7
  12.3 0.0 copy-start.2
  12.3 9.4 %all-to-all-start = ((bf16[16,512,512]{2,1,0:T(8,128)(2,1)}), bf16[16,512,512]{2,1,0:T(8,128)(2,1)}, u32[]{:S(2)}, u32[]{:S(2)}) async-start(bf16[16,512,512]{2,1,0:T(8,128)(2,1)} %stack.8), calls=%async_computation | async-start | bytes 16777216 | tf_op jit(solution)/shard_map/all_to_all | solution.py:69
  21.6 0.0 reduce-scatter.2.cloned.1.call-start
  21.7 0.0 copy-done.7
  21.7 0.0 copy-done.2
  21.7 0.3 broadcast_multiply_fusion
  22.0 0.1 mul.382
  22.2 0.0 copy-start
  22.2 0.0 copy-start.3
  22.2 1.4 fusion.11
  23.6 0.1 reshape.203
  23.7 0.0 copy-done
  23.8 0.5 fusion.8
  24.3 148.6 %all-to-all-done = bf16[16,512,512]{2,1,0:T(8,128)(2,1)} async-done(((bf16[16,512,512]{2,1,0:T(8,128)(2,1)}), bf16[16,512,512]{2,1,0:T(8,128)(2,1)}, u32[]{:S(2)}, u32[]{:S(2)}) %all-to-all-start) | async-done | bytes 8388640 | tf_op jit(solution)/shard_map/all_to_all | solution.py:69
  172.9 0.0 copy-done.3
  172.9 0.0 copy-start.1
  172.9 6.5 %fusion.4 = (f32[128]{0:T(128)S(1)}, f32[128,8192]{1,0:T(8,128)S(1)}) fusion(bf16[128,8192]{1,0:T(8,128)(2,1)S(1)} %copy-done, f32[128]{0:T(128)S(1)} %add_rsqrt_fusion, f32[8192]{0:T(1024)S(1)} %copy-done.3, bf16[128,512]{1,0:T(8,128)(2,1)S(1)} %copy-done.2, bf16[8192,512]{1,0:T(8,128)(2,1)} %bitcast), kind=kOutput, calls=%fused_computation.10 | convolution fusion | flops 1078984576 | bytes 14844928 | tf_op jit(solution)/shard_map/dot_general | solution.py:72
  179.4 0.0 copy-done.1
  179.4 2.5 fusion.7
  181.9 2.5 copy.16
  184.4 3.9 fusion.9
  188.4 4.1 %add_convert_fusion = (bf16[1,256,16,512]{3,1,2,0:T(8,128)(2,1)}, bf16[1,256,16,512]{3,1,2,0:T(8,128)(2,1)S(1)}) fusion(f32[2,256,16,512]{3,1,2,0:T(8,128)S(1)} %fusion.9), kind=kLoop, calls=%fused_computation.3 | loop fusion | flops 8388608 | bytes 25165824 | tf_op jit(solution)/shard_map/convert.3
  192.5 6.5 %copy.19 = bf16[1,256,16,512]{3,2,1,0:T(8,128)(2,1)} copy(bf16[1,256,16,512]{3,1,2,0:T(8,128)(2,1)} %get-tuple-element.11) | data formatting | bytes 8388608 | tf_op jit(solution)/shard_map/convert.3
  199.0 4.3 %copy.20 = bf16[1,256,16,512]{3,2,1,0:T(8,128)(2,1)} copy(bf16[1,256,16,512]{3,1,2,0:T(8,128)(2,1)S(1)} %get-tuple-element.12) | data formatting | bytes 8388608 | tf_op jit(solution)/shard_map/convert.2
  203.3 7.9 %pad_maximum_fusion = bf16[4096,1024]{1,0:T(8,128)(2,1)} fusion(bf16[4096,512]{1,0:T(8,128)(2,1)} %bitcast.28, bf16[4096,512]{1,0:T(8,128)(2,1)} %bitcast.27), kind=kLoop, calls=%fused_computation.1 | loop fusion | flops 16777216 | bytes 16777216 | tf_op jit(solution)/shard_map/concatenate | solution.py:91
  211.2 0.0 copy-start.5
  211.2 0.0 copy-start.6
  211.2 0.0 reduce-scatter.2.cloned.1.call-update
  211.2 131.8 %reduce-scatter.2.cloned.1.call-done = bf16[256,1024]{1,0:T(8,128)(2,1)} async-done(((bf16[4096,1024]{1,0:T(8,128)(2,1)}), bf16[256,1024]{1,0:T(8,128)(2,1)}) %reduce-scatter.2.cloned.1.call-update) | async-done | bytes 524304 | tf_op jit(solution)/shard_map/reduce_scatter | solution.py:92
  343.0 15.2 %all-to-all-start.1 = ((bf16[16,16,1024]{2,1,0:T(8,128)(2,1)}), bf16[16,16,1024]{2,1,0:T(8,128)(2,1)S(1)}, u32[]{:S(2)}, u32[]{:S(2)}) async-start(bf16[16,16,1024]{2,1,0:T(8,128)(2,1)} %bitcast.32), calls=%async_computation.2 | async-start | bytes 1048576 | tf_op jit(solution)/shard_map/all_to_all | solution.py:25
  358.2 13.7 %all-to-all-done.1 = bf16[16,16,1024]{2,1,0:T(8,128)(2,1)S(1)} async-done(((bf16[16,16,1024]{2,1,0:T(8,128)(2,1)}), bf16[16,16,1024]{2,1,0:T(8,128)(2,1)S(1)}, u32[]{:S(2)}, u32[]{:S(2)}) %all-to-all-start.1) | async-done | bytes 524320 | tf_op jit(solution)/shard_map/all_to_all | solution.py:25
  371.9 0.1 convert_reduce_fusion
  372.0 0.0 copy-done.5
  372.0 0.0 copy-done.6
  372.0 0.7 add_divide_fusion
  372.7 1.3 fusion.13
  374.0 0.0 copy-start.4
  374.0 1.3 fusion.12
  375.3 0.0 copy-done.4
  375.3 0.6 fusion.42
  376.0 0.8 broadcast_in_dim.2
  376.8 7.9 %all-to-all-start.2 = ((bf16[16,32,512]{2,1,0:T(8,128)(2,1)}), bf16[16,32,512]{2,1,0:T(8,128)(2,1)S(1)}, u32[]{:S(2)}, u32[]{:S(2)}) async-start(bf16[16,32,512]{2,1,0:T(8,128)(2,1)} %broadcast_in_dim.2), calls=%async_computation.3 | async-start | bytes 1048576 | tf_op jit(solution)/shard_map/all_to_all | solution.py:31
  384.7 5.3 %convolution_convert_fusion = bf16[128,512]{1,0:T(8,128)(2,1)} fusion(bf16[128,8192]{1,0:T(8,128)(2,1)S(1)} %get-tuple-element.14, bf16[8192,512]{1,0:T(8,128)(2,1)} %bitcast), kind=kOutput, calls=%fused_computation.22 | convolution fusion | flops 1073807360 | bytes 10616832 | tf_op jit(solution)/shard_map/dot_general | solution.py:71
  390.0 8.4 %all-to-all-done.2 = bf16[16,32,512]{2,1,0:T(8,128)(2,1)S(1)} async-done(((bf16[16,32,512]{2,1,0:T(8,128)(2,1)}), bf16[16,32,512]{2,1,0:T(8,128)(2,1)S(1)}, u32[]{:S(2)}, u32[]{:S(2)}) %all-to-all-start.2) | async-done | bytes 524320 | tf_op jit(solution)/shard_map/all_to_all | solution.py:31
  398.4 0.8 copy.29
  (11 shorter events, 0.1 us)
Async XLA Ops:
  12.3 9.4 %copy-start.7 = (s32[1024]{0:T(1024)S(1)}, s32[1024]{0:T(1024)}, u32[]{:S(2)}) copy-start(s32[1024]{0:T(1024)} %param.15) | copy-start | bytes 12292
  12.3 9.5 %copy-start.2 = (bf16[128,512]{1,0:T(8,128)(2,1)S(1)}, bf16[128,512]{1,0:T(8,128)(2,1)}, u32[]{:S(2)}) copy-start(bf16[128,512]{1,0:T(8,128)(2,1)} %param.10) | copy-start | bytes 393220
  12.3 160.6 %all-to-all-start = ((bf16[16,512,512]{2,1,0:T(8,128)(2,1)}), bf16[16,512,512]{2,1,0:T(8,128)(2,1)}, u32[]{:S(2)}, u32[]{:S(2)}) async-start(bf16[16,512,512]{2,1,0:T(8,128)(2,1)} %stack.8), calls=%async_computation | async-start | bytes 16777216 | tf_op jit(solution)/shard_map/all_to_all | solution.py:69
  21.6 321.3 %reduce-scatter.2.cloned.1.call-start = ((), (), s32[]{:S(2)}) async-start(), calls=%async_computation.4 | async-start | bytes 8912896 | tf_op jit(solution)/shard_map/reduce_scatter | solution.py:92
  22.2 1.6 copy-start
  22.2 150.7 %copy-start.3 = (f32[8192]{0:T(1024)S(1)}, f32[8192]{0:T(1024)}, u32[]{:S(2)}) copy-start(f32[8192]{0:T(1024)} %param.9) | copy-start | bytes 98308
  172.9 6.5 %copy-start.1 = (bf16[128,8192]{1,0:T(8,128)(2,1)S(1)}, bf16[128,8192]{1,0:T(8,128)(2,1)}, u32[]{:S(2)}) copy-start(bf16[128,8192]{1,0:T(8,128)(2,1)} %param.8) | copy-start | bytes 6291460
  211.2 160.8 %copy-start.5 = (f32[16,1024]{1,0:T(8,128)S(1)}, f32[16,1024]{1,0:T(8,128)}, u32[]{:S(2)}) copy-start(f32[16,1024]{1,0:T(8,128)} %param.13) | copy-start | bytes 196612
  211.2 160.8 %copy-start.6 = (f32[16,1024]{1,0:T(8,128)S(1)}, f32[16,1024]{1,0:T(8,128)}, u32[]{:S(2)}) copy-start(f32[16,1024]{1,0:T(8,128)} %param.14) | copy-start | bytes 196612
  343.0 28.9 %all-to-all-start.1 = ((bf16[16,16,1024]{2,1,0:T(8,128)(2,1)}), bf16[16,16,1024]{2,1,0:T(8,128)(2,1)S(1)}, u32[]{:S(2)}, u32[]{:S(2)}) async-start(bf16[16,16,1024]{2,1,0:T(8,128)(2,1)} %bitcast.32), calls=%async_computation.2 | async-start | bytes 1048576 | tf_op jit(solution)/shard_map/all_to_all | solution.py:25
  374.0 1.3 copy-start.4
  376.8 21.6 %all-to-all-start.2 = ((bf16[16,32,512]{2,1,0:T(8,128)(2,1)}), bf16[16,32,512]{2,1,0:T(8,128)(2,1)S(1)}, u32[]{:S(2)}, u32[]{:S(2)}) async-start(bf16[16,32,512]{2,1,0:T(8,128)(2,1)} %broadcast_in_dim.2), calls=%async_computation.3 | async-start | bytes 1048576 | tf_op jit(solution)/shard_map/all_to_all | solution.py:31
Sparse Core Ops, SparseCore 0:
  211.3 131.6 reduce-scatter.1
